TPU v7x, 256 devices: a whole 4x4x8 slice. The times are simulated.
256 devices in a mesh: dp: 2 (over core), tm: 32 (over z, y), space: 4 (over x).
Axes of the slice: x: 4, y: 4, z: 8, core: 2. Of those that a mesh axis runs over, the one named last changes fastest.
Arguments:
- latents: bfloat16 [2, 64, 8, 80, 512], P('dp', 'tm', 'space'), may hold values from -6 to 6
- norm_gain: float32 [512], replicated, may hold values from 0.25 to 1.75
- kernel: bfloat16 [13824, 512], P(None, 'dp'), may hold values from -0.0546875 to 0.0546875
- conv_bias: float32 [512], replicated, may hold values from -3 to 3
- out_grad: bfloat16 [2, 64, 8, 80, 512], P('dp', 'tm', 'space'), may hold values from -6 to 6
Outputs:
- block_out: bfloat16 [2, 64, 8, 80, 512], P('dp', 'tm', 'space')
- latent_grad: bfloat16 [2, 64, 8, 80, 512], P('dp', 'tm', 'space')
- kernel_grad: float32 [13824, 512], P('tm', 'dp')
- gain_grad: float32 [512], replicated
- bias_grad: float32 [512], replicated
All inputs are finite; a program needn't handle non-finite values.
Results may differ from a plain program's by a relative error of at most 0.0029.
Values may be sent and summed in bfloat16 or wider, within the bound.
No kernel may reach another device: no remote copies, remote signals or barrier semaphores. Data moves between devices by JAX's collectives and lax.ppermute only.
A program may use at most 128 MiB of HBM per device.

v0:
```python
import jax
import jax.numpy as jnp
from jax import lax
from jax.sharding import PartitionSpec as P


def shifted(block, axis, distance):
    devices = range(lax.axis_size(axis))
    route = [(i - distance, i) for i in devices if i - distance in devices]
    return lax.ppermute(block, axis, route)


def padded(block, sides, width):
    for axis, dim in sides:
        count = lax.axis_size(axis)
        forward = [(i, i + 1) for i in range(count - 1)]
        backward = [(target, source) for source, target in forward]
        low = lax.ppermute(
            lax.slice_in_dim(block, block.shape[dim] - width, None, axis=dim), axis, forward
        )
        high = lax.ppermute(lax.slice_in_dim(block, 0, width, axis=dim), axis, backward)
        block = jnp.concatenate([low, block, high], axis=dim)
    return block


def tap_columns(extended, frame_count, row_count, col_count, flipped):
    pieces = []
    for tap_t in range(3):
        for tap_h in range(3):
            for tap_w in range(3):
                if flipped:
                    start_t, start_h, start_w = (2 - tap_t, 2 - tap_h, 2 - tap_w)
                else:
                    start_t, start_h, start_w = (tap_t, tap_h, tap_w)
                pieces.append(
                    extended[
                        :,
                        start_t : start_t + frame_count,
                        start_h : start_h + row_count,
                        start_w : start_w + col_count,
                        :,
                    ]
                )
    stacked = jnp.concatenate(pieces, axis=-1)
    return stacked.reshape(-1, stacked.shape[-1])


def pad_columns(extended):
    return jnp.pad(extended, ((0, 0), (0, 0), (0, 0), (1, 1), (0, 0)))


def on_device(latents, norm_gain, kernel, conv_bias, out_grad):
    chans = latents.shape[-1]
    half_cols = kernel.shape[1]
    clip_local, frame_count, row_count, col_count = (
        latents.shape[0],
        latents.shape[1],
        latents.shape[2],
        latents.shape[3],
    )
    cell_total = (
        clip_local
        * frame_count
        * row_count
        * col_count
        * lax.axis_size("dp")
        * lax.axis_size("tm")
        * lax.axis_size("space")
    )
    grad_scale = 1.0 / jnp.sqrt(jnp.float32(cell_total))
    floats = latents.astype(jnp.float32)
    scale = lax.rsqrt(jnp.mean(floats * floats, axis=-1, keepdims=True) + 1e-06)
    normed = floats * scale
    pre_act = normed * norm_gain
    act = jax.nn.silu(pre_act).astype(jnp.bfloat16)
    grad_pair = lax.all_to_all(out_grad, "dp", split_axis=4, concat_axis=0, tiled=True)
    earlier = shifted(act, "tm", 1)
    joined = jnp.concatenate([earlier, act], axis=1)
    act_ext = padded(joined, (("space", 2),), 1)
    later = shifted(grad_pair, "tm", -1)
    joined_grad = jnp.concatenate([grad_pair, later], axis=1)
    grad_ext = padded(joined_grad, (("space", 2),), 1)
    act_pair = lax.all_gather(act_ext, "dp", axis=0, tiled=True)
    pair_clips = act_pair.shape[0]
    act_taps = tap_columns(pad_columns(act_pair), frame_count, row_count, col_count, False)
    conv_part = jnp.dot(act_taps, kernel, preferred_element_type=jnp.float32)
    conv_part = conv_part.reshape(pair_clips, frame_count, row_count, col_count, half_cols)
    conv = lax.all_to_all(conv_part, "dp", split_axis=0, concat_axis=4, tiled=True)
    block_out = (floats + conv + conv_bias).astype(jnp.bfloat16)
    kernel_local = (
        lax.dot_general(
            act_taps,
            grad_pair.reshape(-1, half_cols),
            (((0,), (0,)), ((), ())),
            preferred_element_type=jnp.float32,
        )
        * grad_scale
    )
    flipped_kernel = jnp.transpose(kernel.reshape(-1, chans, half_cols), (0, 2, 1)).reshape(
        -1, chans
    )
    grad_taps = tap_columns(pad_columns(grad_ext), frame_count, row_count, col_count, True)
    partial_grad = jnp.dot(grad_taps, flipped_kernel, preferred_element_type=jnp.float32)
    partial_grad = partial_grad.reshape(pair_clips, frame_count, row_count, col_count, chans)
    act_grad = lax.psum_scatter(partial_grad, "dp", scatter_dimension=0, tiled=True)
    grads = out_grad.astype(jnp.float32)
    bias_local = jnp.sum(grads.reshape(-1, chans), axis=0) * grad_scale
    sig = jax.nn.sigmoid(pre_act)
    pre_grad = act_grad * sig * (1.0 + pre_act * (1.0 - sig))
    gain_local = jnp.sum((pre_grad * normed).reshape(-1, chans), axis=0) * grad_scale
    normed_grad = pre_grad * norm_gain
    latent_grad = grads + scale * (
        normed_grad - normed * jnp.mean(normed_grad * normed, axis=-1, keepdims=True)
    )
    gain_grad, bias_grad = lax.psum((gain_local, bias_local), ("dp", "tm", "space"))
    row_part = lax.psum_scatter(kernel_local, "tm", scatter_dimension=0, tiled=True)
    kernel_grad = lax.psum(row_part, "space")
    return (block_out, latent_grad.astype(jnp.bfloat16), kernel_grad, gain_grad, bias_grad)


def solution(mesh):
    in_specs = (
        P("dp", "tm", "space", None, None),
        P(),
        P(None, "dp"),
        P(),
        P("dp", "tm", "space", None, None),
    )
    out_specs = (
        P("dp", "tm", "space", None, None),
        P("dp", "tm", "space", None, None),
        P("tm", "dp"),
        P(),
        P(),
    )
    return jax.shard_map(
        on_device, mesh=mesh, in_specs=in_specs, out_specs=out_specs, check_vma=False
    )
```

profile of v0, /device:TPU:8, one launch (start us, length us, event | category | flops | bytes accessed | tf_op | source)
XLA Modules:
  0.0 441.9 jit_solution(11372110334327910266)
XLA Ops:
  7.2 1.3 copy.20
  8.5 4.2 all_to_all.36
  13.0 4.1 collective-permute-start.3
  17.1 7.6 %collective-permute-done.3 = bf16[2,2,2,80,256]{4,3,2,1,0:T(8,128)(2,1)S(1)} collective-permute-done((bf16[2,2,2,80,256]{4,3,2,1,0:T(8,128)(2,1)S(1)}, bf16[2,2,2,80,256]{4,3,2,1,0:T(8,128)(2,1)S(1)}, u32[]{:S(2)}, u32[]{:S(2)}) %collective-permute-start.3) | collective-permute-done | bytes 327712 | tf_op jit(solution)/shard_map/ppermute | solution.py:10
  24.7 3.4 collective-permute-start.4
  28.2 1.3 collective-permute-start.5
  29.5 10.3 %copy.23 = bf16[27,256,512]{2,1,0:T(8,128)(2,1)} copy(bf16[27,256,512]{1,2,0:T(8,128)(2,1)} %bitcast.37) | data formatting | bytes 14155776 | tf_op jit(solution)/shard_map/transpose | solution.py:99
  42.0 0.9 slice-done
  42.9 1.1 slice-done.1
  44.0 5.8 %fusion.31 = f32[2,2,2,80,512]{4,3,2,1,0:T(8,128)} fusion(bf16[2,2,2,80,6912]{4,3,2,1,0:T(8,128)(2,1)S(1)} %slice_dynamic-update-slice_fusion.27, bf16[6912,512,1,1,1]{1,0,4,3,2:T(8,128)(2,1)S(1)} %bitcast.40), kind=kOutput, calls=%fused_computation.109 | convolution fusion | flops 4529848320 | bytes 17235968 | tf_op jit(solution)/shard_map/dot_general | solution.py:103
  50.1 20.0 %reduce-scatter.3.cloned.1.call-done = f32[1,2,2,80,512]{4,3,2,1,0:T(8,128)} async-done(((f32[2,2,2,80,512]{4,3,2,1,0:T(8,128)}), f32[1,2,2,80,512]{4,3,2,1,0:T(8,128)}) %reduce-scatter.3.cloned.1.call-update) | async-done | bytes 655376 | tf_op jit(solution)/shard_map/reduce_scatter | solution.py:105
  70.1 1.6 fusion.23
  71.7 2.4 fusion.13
  74.1 3.4 collective-permute-start
  77.5 8.2 %collective-permute-done = bf16[1,2,2,80,512]{4,3,2,1,0:T(8,128)(2,1)S(1)} collective-permute-done((bf16[1,2,2,80,512]{4,3,2,1,0:T(8,128)(2,1)S(1)}, bf16[1,2,2,80,512]{4,3,2,1,0:T(8,128)(2,1)S(1)}, u32[]{:S(2)}, u32[]{:S(2)}) %collective-permute-start) | collective-permute-done | bytes 327712 | tf_op jit(solution)/shard_map/ppermute | solution.py:10
  85.8 3.4 collective-permute-start.1
  89.2 1.3 collective-permute-start.2
  90.5 5.1 %collective-permute-done.1 = bf16[1,4,1,80,512]{4,3,2,1,0:T(8,128)(2,1)S(1)} collective-permute-done((bf16[1,4,1,80,512]{4,3,2,1,0:T(8,128)(2,1)S(1)}, bf16[1,4,1,80,512]{4,3,2,1,0:T(8,128)(2,1)S(1)}, u32[]{:S(2)}, u32[]{:S(2)}) %collective-permute-start.1) | collective-permute-done | bytes 327712 | tf_op jit(solution)/shard_map/ppermute | solution.py:18
  95.6 4.1 collective-permute-done.2
  99.7 1.2 pad_maximum_fusion
  101.2 18.5 %all-gather.2.cloned.1.call-done = bf16[2,4,4,80,512]{4,3,2,1,0:T(8,128)(2,1)} async-done(((bf16[1,4,4,80,512]{4,3,2,1,0:T(8,128)(2,1)}), bf16[2,4,4,80,512]{4,3,2,1,0:T(8,128)(2,1)}) %all-gather.2.cloned.1.call-update) | async-done | bytes 2621456 | tf_op jit(solution)/shard_map/all_gather | solution.py:83
  119.7 1.4 slice_dynamic-update-slice_fusion.26
  121.0 1.1 slice_dynamic-update-slice_fusion.8
  122.2 1.2 slice_dynamic-update-slice_fusion.25
  126.4 6.1 %copy-done.3 = bf16[2,2,2,80,13824]{4,3,2,1,0:T(8,128)(2,1)} copy-done((bf16[2,2,2,80,13824]{4,3,2,1,0:T(8,128)(2,1)}, bf16[2,2,2,80,13824]{4,3,2,1,0:T(8,128)(2,1)S(1)}, u32[]{:S(2)}) %copy-start.3) | copy-done | bytes 17694744
  132.5 9.0 %convolution_multiply_fusion = f32[13824,256]{1,0:T(8,128)} fusion(bf16[640,13824]{1,0:T(8,128)(2,1)S(1)} %bitcast.44, bf16[640,256]{1,0:T(8,128)(2,1)S(1)} %bitcast.36), kind=kOutput, calls=%fused_computation | convolution fusion | flops 4533387264 | bytes 32178176 | tf_op jit(solution)/shard_map/dot_general | solution.py:91
  141.6 77.4 %all-reduce.2 = (f32[512]{0:T(512)}, f32[512]{0:T(512)}) all-reduce(f32[512]{0:T(512)S(1)} %broadcast_multiply_fusion.1, f32[512]{0:T(512)S(1)} %broadcast_multiply_fusion), channel_id=1, replica_groups=mesh['dp'=2,'tm'=32,'space'=4] {'dp','tm','space'}, use_global_device_ids=true, to_apply=%region_6.7 | all-reduce | flops 1024 | bytes 8192 | tf_op jit(solution)/shard_map/psum | solution.py:115
  219.0 165.6 %reduce-scatter.5.cloned.1.call-done = f32[432,256]{1,0:T(8,128)} async-done(((f32[13824,256]{1,0:T(8,128)}), f32[432,256]{1,0:T(8,128)}) %reduce-scatter.5.cloned.1.call-update) | async-done | bytes 442384 | tf_op jit(solution)/shard_map/reduce_scatter | solution.py:116
  384.6 10.5 %fusion = f32[2,2,2,80,256]{4,3,2,1,0:T(8,128)S(1)} fusion(bf16[2,2,2,80,13824]{4,3,2,1,0:T(8,128)(2,1)} %copy-done.3, bf16[13824,256]{1,0:T(8,128)(2,1)} %param.7), kind=kOutput, calls=%fused_computation.1 | convolution fusion | flops 4529848320 | bytes 25427968 | tf_op jit(solution)/shard_map/dot_general | solution.py:86
  395.2 4.3 all_to_all.37
  400.3 33.2 %all-reduce.5.cloned.1.call-done = f32[432,256]{1,0:T(8,128)} async-done(((f32[432,256]{1,0:T(8,128)}), f32[432,256]{1,0:T(8,128)}) %all-reduce.5.cloned.1.call-update) | async-done | bytes 442384 | tf_op jit(solution)/shard_map/psum | solution.py:117
  433.5 1.8 copy.82
  (87 shorter events, 6.8 us)
Async XLA Ops:
  7.2 62.9 %reduce-scatter.3.cloned.1.call-start = ((), (), s32[]{:S(2)}) async-start(), calls=%async_computation.5 | async-start | bytes 1966080 | tf_op jit(solution)/shard_map/reduce_scatter | solution.py:105
  13.0 11.6 %collective-permute-start.3 = (bf16[2,2,2,80,256]{4,3,2,1,0:T(8,128)(2,1)S(1)}, bf16[2,2,2,80,256]{4,3,2,1,0:T(8,128)(2,1)S(1)}, u32[]{:S(2)}, u32[]{:S(2)}) collective-permute-start(bf16[2,2,2,80,256]{4,3,2,1,0:T(8,128)(2,1)S(1)} %bitcast.31), channel_id=1, source_target_pairs={{4,0},{8,4},{12,8},{16,12},{20,16},{24,20},{28,24},{32,28},{36,32}... | collective-permute-start | bytes 983048 | tf_op jit(solution)/shard_map/ppermute | solution.py:10
  24.7 15.0 %collective-permute-start.4 = (bf16[2,4,1,80,256]{4,3,2,1,0:T(8,128)(2,1)S(1)}, bf16[2,4,1,80,256]{4,3,2,1,0:T(8,128)(2,1)S(1)}, u32[]{:S(2)}, u32[]{:S(2)}) collective-permute-start(bf16[2,4,1,80,256]{4,3,2,1,0:T(8,128)(2,1)S(1)} %get-tuple-element.11), channel_id=1, source_target_pairs={{0,1},{1,2},{2,3},{4,5},{5,6},{6,7},{8,9},{9,10},{10,11},{12,13},{... | collective-permute-start | bytes 983048 | tf_op jit(solution)/shard_map/ppermute | solution.py:18
  28.2 11.6 %collective-permute-start.5 = (bf16[2,4,1,80,256]{4,3,2,1,0:T(8,128)(2,1)S(1)}, bf16[2,4,1,80,256]{4,3,2,1,0:T(8,128)(2,1)S(1)}, u32[]{:S(2)}, u32[]{:S(2)}) collective-permute-start(bf16[2,4,1,80,256]{4,3,2,1,0:T(8,128)(2,1)S(1)} %get-tuple-element.12), channel_id=1, source_target_pairs={{1,0},{2,1},{3,2},{5,4},{6,5},{7,6},{9,8},{10,9},{11,10},{13,12},{... | collective-permute-start | bytes 983048 | tf_op jit(solution)/shard_map/ppermute | solution.py:21
  40.7 2.2 slice-start
  41.4 2.6 slice-start.1
  44.0 5.9 %copy-start.1 = (bf16[1,2,2,80,512]{4,3,2,1,0:T(8,128)(2,1)S(1)}, bf16[1,2,2,80,512]{4,3,2,1,0:T(8,128)(2,1)}, u32[]{:S(2)}) copy-start(bf16[1,2,2,80,512]{4,3,2,1,0:T(8,128)(2,1)} %param.5) | copy-start | bytes 983044
  44.0 26.1 %copy-start.4 = (f32[512]{0:T(512)S(1)}, f32[512]{0:T(512)}, u32[]{:S(2)}) copy-start(f32[512]{0:T(512)} %param.6) | copy-start | bytes 6148
  44.0 27.7 %copy-start.2 = (bf16[1,2,2,80,512]{4,3,2,1,0:T(8,128)(2,1)S(1)}, bf16[1,2,2,80,512]{4,3,2,1,0:T(8,128)(2,1)}, u32[]{:S(2)}) copy-start(bf16[1,2,2,80,512]{4,3,2,1,0:T(8,128)(2,1)} %param.9) | copy-start | bytes 983044
  49.8 69.8 %all-gather.2.cloned.1.call-start = ((), (), s32[]{:S(2)}) async-start(), calls=%async_computation.4 | async-start | bytes 3932160 | tf_op jit(solution)/shard_map/all_gather | solution.py:83
  74.1 11.6 %collective-permute-start = (bf16[1,2,2,80,512]{4,3,2,1,0:T(8,128)(2,1)S(1)}, bf16[1,2,2,80,512]{4,3,2,1,0:T(8,128)(2,1)S(1)}, u32[]{:S(2)}, u32[]{:S(2)}) collective-permute-start(bf16[1,2,2,80,512]{4,3,2,1,0:T(8,128)(2,1)S(1)} %get-tuple-element.16), channel_id=1, source_target_pairs={{0,4},{4,8},{8,12},{12,16},{16,20},{20,24},{24,28},{28,32},{32,36}... | collective-permute-start | bytes 983048 | tf_op jit(solution)/shard_map/ppermute | solution.py:10
  85.8 9.8 %collective-permute-start.1 = (bf16[1,4,1,80,512]{4,3,2,1,0:T(8,128)(2,1)S(1)}, bf16[1,4,1,80,512]{4,3,2,1,0:T(8,128)(2,1)S(1)}, u32[]{:S(2)}, u32[]{:S(2)}) collective-permute-start(bf16[1,4,1,80,512]{4,3,2,1,0:T(8,128)(2,1)S(1)} %get-tuple-element.13), channel_id=1, source_target_pairs={{0,1},{1,2},{2,3},{4,5},{5,6},{6,7},{8,9},{9,10},{10,11},{12,13},{... | collective-permute-start | bytes 983048 | tf_op jit(solution)/shard_map/ppermute | solution.py:18
  89.2 10.5 %collective-permute-start.2 = (bf16[1,4,1,80,512]{4,3,2,1,0:T(8,128)(2,1)S(1)}, bf16[1,4,1,80,512]{4,3,2,1,0:T(8,128)(2,1)S(1)}, u32[]{:S(2)}, u32[]{:S(2)}) collective-permute-start(bf16[1,4,1,80,512]{4,3,2,1,0:T(8,128)(2,1)S(1)} %get-tuple-element.14), channel_id=1, source_target_pairs={{1,0},{2,1},{3,2},{5,4},{6,5},{7,6},{9,8},{10,9},{11,10},{13,12},{... | collective-permute-start | bytes 983048 | tf_op jit(solution)/shard_map/ppermute | solution.py:21
  101.0 283.7 %reduce-scatter.5.cloned.1.call-start = ((), (), s32[]{:S(2)}) async-start(), calls=%async_computation.6 | async-start | bytes 14598144 | tf_op jit(solution)/shard_map/reduce_scatter | solution.py:116
  119.6 3.8 copy-start
  126.4 6.1 %copy-start.3 = (bf16[2,2,2,80,13824]{4,3,2,1,0:T(8,128)(2,1)}, bf16[2,2,2,80,13824]{4,3,2,1,0:T(8,128)(2,1)S(1)}, u32[]{:S(2)}) copy-start(bf16[2,2,2,80,13824]{4,3,2,1,0:T(8,128)(2,1)S(1)} %slice_dynamic-update-slice_fusion.9) | copy-start | bytes 53084164
  141.5 292.0 %all-reduce.5.cloned.1.call-start = ((), (), s32[]{:S(2)}) async-start(), calls=%async_computation.7 | async-start | bytes 884736 | tf_op jit(solution)/shard_map/psum | solution.py:117
  384.6 14.9 %copy-start.5 = (f32[512]{0:T(512)S(1)}, f32[512]{0:T(512)}, u32[]{:S(2)}) copy-start(f32[512]{0:T(512)} %param.8) | copy-start | bytes 6148
Sparse Core Ops, SparseCore 0:
  50.0 20.0 reduce-scatter.2
  101.1 18.5 all-gather.1
  141.6 242.9 reduce-scatter.4
  386.8 46.6 all-reduce.4
where the time goes:
time: 443 us; the launch traced here: 442 us
  waiting for transfers between devices  262 us (59%)
  blocking collectives  85.8 us (19%)
  local copies, waits for them, and re-layouts  29.6 us (7%)
  matrix products  25.3 us (6%)
  starting transfers between devices  17.2 us (4%)
  between operations  14.4 us (3%)
  other arithmetic  7.21 us (2%)
    reduce_scatter x1, waiting for transfers between devices, on_device(): lax.psum_scatter(kernel_local, 'tm', scatter_dimension=0, tiled=True)  166 us
    psum x1, blocking collectives, on_device(): lax.psum((gain_local, bias_local), ('dp', 'tm', 'space'))  77.4 us
    psum x1, waiting for transfers between devices, on_device(): kernel_grad = lax.psum(row_part, 'space')  33.2 us
    reduce_scatter x1, waiting for transfers between devices, on_device(): lax.psum_scatter(partial_grad, 'dp', scatter_dimension=0, tiled=True)  20 us
    unnamed x69, local copies, waits for them, and re-layouts  18.6 us
    all_gather x1, waiting for transfers between devices, on_device(): act_pair = lax.all_gather(act_ext, 'dp', axis=0, tiled=True)  18.5 us
    ppermute x2, waiting for transfers between devices, shifted(): return lax.ppermute(block, axis, route)  15.8 us
    dot_general x1, matrix products, on_device(): conv_part = jnp.dot(act_taps, kernel, preferred_element_type=jnp.float32)  10.5 us
  transfers between devices with their start and end apart: 10, of which 8 were waited for; matrix products, arithmetic and copies ran while one was open for 5% of the time, Pallas kernels for 0%

commit v1 on v0

--- a/solution.py
+++ b/solution.py
@@ -2,6 +2,14 @@
 import jax.numpy as jnp
 from jax import lax
 from jax.sharding import PartitionSpec as P
+
+
+def added_up(x, axis):
+    size, total = (lax.axis_size(axis), x)
+    for reach in [1 << k for k in range(size.bit_length() - 1)]:
+        swap = [(i, i ^ reach) for i in range(size)]
+        total = total + lax.ppermute(total, axis, swap)
+    return total
 
 
 def shifted(block, axis, distance):
@@ -114,7 +122,7 @@
     )
     gain_grad, bias_grad = lax.psum((gain_local, bias_local), ("dp", "tm", "space"))
     row_part = lax.psum_scatter(kernel_local, "tm", scatter_dimension=0, tiled=True)
-    kernel_grad = lax.psum(row_part, "space")
+    kernel_grad = added_up(row_part, "space")
     return (block_out, latent_grad.astype(jnp.bfloat16), kernel_grad, gain_grad, bias_grad)
 
 

time: 443 us -> 489 us (1.10)
  waiting for transfers between devices: 262 us -> 307 us
    reduce_scatter x1, waiting for transfers between devices: 166 us -> 243 us  [on_device(): lax.psum_scatter(kernel_local, 'tm', scatter_dimension=0, tiled=True)]
    psum x1 -> x0, waiting for transfers between devices: 33.2 us -> none  [on_device(): kernel_grad = lax.psum(row_part, 'space')]
    unnamed x69 -> x68, local copies, waits for them, and re-layouts: 18.6 us -> 16.8 us
  transfers between devices with their start and end apart: 10 -> 11, of which waited for: 8 -> 7; matrix products, arithmetic and copies ran while one was open for 5% -> 5% of each run, Pallas kernels for 0% -> 0%
where the time goes in v1:
time: 489 us; the launch traced here: 486 us
  waiting for transfers between devices  307 us (63%)
  blocking collectives  82.2 us (17%)
  local copies, waits for them, and re-layouts  27.8 us (6%)
  matrix products  25.3 us (5%)
  starting transfers between devices  20.8 us (4%)
  between operations  14.3 us (3%)
  other arithmetic  9.1 us (2%)
    reduce_scatter x1, waiting for transfers between devices, on_device(): lax.psum_scatter(kernel_local, 'tm', scatter_dimension=0, tiled=True)  243 us
    psum x1, blocking collectives, on_device(): lax.psum((gain_local, bias_local), ('dp', 'tm', 'space'))  73.8 us
    reduce_scatter x1, waiting for transfers between devices, on_device(): lax.psum_scatter(partial_grad, 'dp', scatter_dimension=0, tiled=True)  20 us
    all_gather x1, waiting for transfers between devices, on_device(): act_pair = lax.all_gather(act_ext, 'dp', axis=0, tiled=True)  18.5 us
    unnamed x68, local copies, waits for them, and re-layouts  16.8 us
    ppermute x2, waiting for transfers between devices, shifted(): return lax.ppermute(block, axis, route)  15.8 us
    dot_general x1, matrix products, on_device(): conv_part = jnp.dot(act_taps, kernel, preferred_element_type=jnp.float32)  10.5 us
    transpose x1, local copies, waits for them, and re-layouts, on_device(): jnp.transpose(kernel.reshape(-1, chans, half_cols), (0, 2, 1))  10.3 us
  transfers between devices with their start and end apart: 11, of which 7 were waited for; matrix products, arithmetic and copies ran while one was open for 5% of the time, Pallas kernels for 0%

profile of v1, /device:TPU:8, one launch (start us, length us, event | category | flops | bytes accessed | tf_op | source)
XLA Modules:
  0.0 486.0 jit_solution(14266272378136626255)
XLA Ops:
  7.2 1.3 copy.20
  8.5 4.2 all_to_all.36
  13.0 4.1 collective-permute-start.3
  17.1 7.6 %collective-permute-done.3 = bf16[2,2,2,80,256]{4,3,2,1,0:T(8,128)(2,1)S(1)} collective-permute-done((bf16[2,2,2,80,256]{4,3,2,1,0:T(8,128)(2,1)S(1)}, bf16[2,2,2,80,256]{4,3,2,1,0:T(8,128)(2,1)S(1)}, u32[]{:S(2)}, u32[]{:S(2)}) %collective-permute-start.3) | collective-permute-done | bytes 327712 | tf_op jit(solution)/shard_map/ppermute | solution.py:18
  24.7 3.4 collective-permute-start.4
  28.2 1.3 collective-permute-start.5
  29.5 10.3 %copy.23 = bf16[27,256,512]{2,1,0:T(8,128)(2,1)} copy(bf16[27,256,512]{1,2,0:T(8,128)(2,1)} %bitcast.37) | data formatting | bytes 14155776 | tf_op jit(solution)/shard_map/transpose | solution.py:107
  42.9 1.1 slice-done.1
  44.0 5.8 %fusion.31 = f32[2,2,2,80,512]{4,3,2,1,0:T(8,128)} fusion(bf16[2,2,2,80,6912]{4,3,2,1,0:T(8,128)(2,1)S(1)} %slice_dynamic-update-slice_fusion.27, bf16[6912,512,1,1,1]{1,0,4,3,2:T(8,128)(2,1)S(1)} %bitcast.40), kind=kOutput, calls=%fused_computation.109 | convolution fusion | flops 4529848320 | bytes 17235968 | tf_op jit(solution)/shard_map/dot_general | solution.py:111
  50.1 20.0 %reduce-scatter.3.cloned.1.call-done = f32[1,2,2,80,512]{4,3,2,1,0:T(8,128)} async-done(((f32[2,2,2,80,512]{4,3,2,1,0:T(8,128)}), f32[1,2,2,80,512]{4,3,2,1,0:T(8,128)}) %reduce-scatter.3.cloned.1.call-update) | async-done | bytes 655376 | tf_op jit(solution)/shard_map/reduce_scatter | solution.py:113
  70.1 1.6 fusion.23
  71.7 2.4 fusion.13
  74.1 3.4 collective-permute-start
  77.5 8.2 %collective-permute-done = bf16[1,2,2,80,512]{4,3,2,1,0:T(8,128)(2,1)S(1)} collective-permute-done((bf16[1,2,2,80,512]{4,3,2,1,0:T(8,128)(2,1)S(1)}, bf16[1,2,2,80,512]{4,3,2,1,0:T(8,128)(2,1)S(1)}, u32[]{:S(2)}, u32[]{:S(2)}) %collective-permute-start) | collective-permute-done | bytes 327712 | tf_op jit(solution)/shard_map/ppermute | solution.py:18
  85.8 3.4 collective-permute-start.1
  89.2 1.3 collective-permute-start.2
  90.5 5.1 %collective-permute-done.1 = bf16[1,4,1,80,512]{4,3,2,1,0:T(8,128)(2,1)S(1)} collective-permute-done((bf16[1,4,1,80,512]{4,3,2,1,0:T(8,128)(2,1)S(1)}, bf16[1,4,1,80,512]{4,3,2,1,0:T(8,128)(2,1)S(1)}, u32[]{:S(2)}, u32[]{:S(2)}) %collective-permute-start.1) | collective-permute-done | bytes 327712 | tf_op jit(solution)/shard_map/ppermute | solution.py:26
  95.6 4.1 collective-permute-done.2
  99.7 1.2 pad_maximum_fusion
  101.2 18.5 %all-gather.2.cloned.1.call-done = bf16[2,4,4,80,512]{4,3,2,1,0:T(8,128)(2,1)} async-done(((bf16[1,4,4,80,512]{4,3,2,1,0:T(8,128)(2,1)}), bf16[2,4,4,80,512]{4,3,2,1,0:T(8,128)(2,1)}) %all-gather.2.cloned.1.call-update) | async-done | bytes 2621456 | tf_op jit(solution)/shard_map/all_gather | solution.py:91
  119.6 1.4 slice_dynamic-update-slice_fusion.26
  121.0 1.1 slice_dynamic-update-slice_fusion.8
  122.2 1.2 slice_dynamic-update-slice_fusion.25
  126.4 6.1 %copy-done.3 = bf16[2,2,2,80,13824]{4,3,2,1,0:T(8,128)(2,1)} copy-done((bf16[2,2,2,80,13824]{4,3,2,1,0:T(8,128)(2,1)}, bf16[2,2,2,80,13824]{4,3,2,1,0:T(8,128)(2,1)S(1)}, u32[]{:S(2)}) %copy-start.3) | copy-done | bytes 17694744
  132.5 9.0 %convolution_multiply_fusion = f32[13824,256]{1,0:T(8,128)} fusion(bf16[640,13824]{1,0:T(8,128)(2,1)S(1)} %bitcast.44, bf16[640,256]{1,0:T(8,128)(2,1)S(1)} %bitcast.36), kind=kOutput, calls=%fused_computation | convolution fusion | flops 4533387264 | bytes 32178176 | tf_op jit(solution)/shard_map/dot_general | solution.py:99
  141.5 243.0 %reduce-scatter.5.cloned.1.call-done = f32[432,256]{1,0:T(8,128)} async-done(((f32[13824,256]{1,0:T(8,128)}), f32[432,256]{1,0:T(8,128)}) %reduce-scatter.5.cloned.1.call-update) | async-done | bytes 442384 | tf_op jit(solution)/shard_map/reduce_scatter | solution.py:124
  384.4 1.8 collective-permute-start.6
  386.2 73.8 %all-reduce.2 = (f32[512]{0:T(512)}, f32[512]{0:T(512)}) all-reduce(f32[512]{0:T(512)S(1)} %broadcast_multiply_fusion.1, f32[512]{0:T(512)S(1)} %broadcast_multiply_fusion), channel_id=1, replica_groups=mesh['dp'=2,'tm'=32,'space'=4] {'dp','tm','space'}, use_global_device_ids=true, to_apply=%region_5.6 | all-reduce | flops 1024 | bytes 8192 | tf_op jit(solution)/shard_map/psum | solution.py:123
  460.0 1.1 add.59
  461.0 1.9 collective-permute-start.7
  462.9 10.5 %fusion = f32[2,2,2,80,256]{4,3,2,1,0:T(8,128)S(1)} fusion(bf16[2,2,2,80,13824]{4,3,2,1,0:T(8,128)(2,1)} %copy-done.3, bf16[13824,256]{1,0:T(8,128)(2,1)} %param.7), kind=kOutput, calls=%fused_computation.1 | convolution fusion | flops 4529848320 | bytes 25427968 | tf_op jit(solution)/shard_map/dot_general | solution.py:94
  473.4 4.3 all_to_all.37
  (89 shorter events, 8.5 us)
Async XLA Ops:
  7.2 62.9 %reduce-scatter.3.cloned.1.call-start = ((), (), s32[]{:S(2)}) async-start(), calls=%async_computation.5 | async-start | bytes 1966080 | tf_op jit(solution)/shard_map/reduce_scatter | solution.py:113
  13.0 11.6 %collective-permute-start.3 = (bf16[2,2,2,80,256]{4,3,2,1,0:T(8,128)(2,1)S(1)}, bf16[2,2,2,80,256]{4,3,2,1,0:T(8,128)(2,1)S(1)}, u32[]{:S(2)}, u32[]{:S(2)}) collective-permute-start(bf16[2,2,2,80,256]{4,3,2,1,0:T(8,128)(2,1)S(1)} %bitcast.31), channel_id=1, source_target_pairs={{4,0},{8,4},{12,8},{16,12},{20,16},{24,20},{28,24},{32,28},{36,32}... | collective-permute-start | bytes 983048 | tf_op jit(solution)/shard_map/ppermute | solution.py:18
  24.7 15.0 %collective-permute-start.4 = (bf16[2,4,1,80,256]{4,3,2,1,0:T(8,128)(2,1)S(1)}, bf16[2,4,1,80,256]{4,3,2,1,0:T(8,128)(2,1)S(1)}, u32[]{:S(2)}, u32[]{:S(2)}) collective-permute-start(bf16[2,4,1,80,256]{4,3,2,1,0:T(8,128)(2,1)S(1)} %get-tuple-element.11), channel_id=1, source_target_pairs={{0,1},{1,2},{2,3},{4,5},{5,6},{6,7},{8,9},{9,10},{10,11},{12,13},{... | collective-permute-start | bytes 983048 | tf_op jit(solution)/shard_map/ppermute | solution.py:26
  28.2 11.6 %collective-permute-start.5 = (bf16[2,4,1,80,256]{4,3,2,1,0:T(8,128)(2,1)S(1)}, bf16[2,4,1,80,256]{4,3,2,1,0:T(8,128)(2,1)S(1)}, u32[]{:S(2)}, u32[]{:S(2)}) collective-permute-start(bf16[2,4,1,80,256]{4,3,2,1,0:T(8,128)(2,1)S(1)} %get-tuple-element.12), channel_id=1, source_target_pairs={{1,0},{2,1},{3,2},{5,4},{6,5},{7,6},{9,8},{10,9},{11,10},{13,12},{... | collective-permute-start | bytes 983048 | tf_op jit(solution)/shard_map/ppermute | solution.py:29
  40.7 2.2 slice-start
  41.4 2.6 slice-start.1
  44.0 5.9 %copy-start.1 = (bf16[1,2,2,80,512]{4,3,2,1,0:T(8,128)(2,1)S(1)}, bf16[1,2,2,80,512]{4,3,2,1,0:T(8,128)(2,1)}, u32[]{:S(2)}) copy-start(bf16[1,2,2,80,512]{4,3,2,1,0:T(8,128)(2,1)} %param.5) | copy-start | bytes 983044
  44.0 26.1 %copy-start.4 = (f32[512]{0:T(512)S(1)}, f32[512]{0:T(512)}, u32[]{:S(2)}) copy-start(f32[512]{0:T(512)} %param.6) | copy-start | bytes 6148
  44.0 27.7 %copy-start.2 = (bf16[1,2,2,80,512]{4,3,2,1,0:T(8,128)(2,1)S(1)}, bf16[1,2,2,80,512]{4,3,2,1,0:T(8,128)(2,1)}, u32[]{:S(2)}) copy-start(bf16[1,2,2,80,512]{4,3,2,1,0:T(8,128)(2,1)} %param.9) | copy-start | bytes 983044
  49.8 69.8 %all-gather.2.cloned.1.call-start = ((), (), s32[]{:S(2)}) async-start(), calls=%async_computation.4 | async-start | bytes 3932160 | tf_op jit(solution)/shard_map/all_gather | solution.py:91
  74.1 11.6 %collective-permute-start = (bf16[1,2,2,80,512]{4,3,2,1,0:T(8,128)(2,1)S(1)}, bf16[1,2,2,80,512]{4,3,2,1,0:T(8,128)(2,1)S(1)}, u32[]{:S(2)}, u32[]{:S(2)}) collective-permute-start(bf16[1,2,2,80,512]{4,3,2,1,0:T(8,128)(2,1)S(1)} %get-tuple-element.16), channel_id=1, source_target_pairs={{0,4},{4,8},{8,12},{12,16},{16,20},{20,24},{24,28},{28,32},{32,36}... | collective-permute-start | bytes 983048 | tf_op jit(solution)/shard_map/ppermute | solution.py:18
  85.8 9.8 %collective-permute-start.1 = (bf16[1,4,1,80,512]{4,3,2,1,0:T(8,128)(2,1)S(1)}, bf16[1,4,1,80,512]{4,3,2,1,0:T(8,128)(2,1)S(1)}, u32[]{:S(2)}, u32[]{:S(2)}) collective-permute-start(bf16[1,4,1,80,512]{4,3,2,1,0:T(8,128)(2,1)S(1)} %get-tuple-element.13), channel_id=1, source_target_pairs={{0,1},{1,2},{2,3},{4,5},{5,6},{6,7},{8,9},{9,10},{10,11},{12,13},{... | collective-permute-start | bytes 983048 | tf_op jit(solution)/shard_map/ppermute | solution.py:26
  89.2 10.5 %collective-permute-start.2 = (bf16[1,4,1,80,512]{4,3,2,1,0:T(8,128)(2,1)S(1)}, bf16[1,4,1,80,512]{4,3,2,1,0:T(8,128)(2,1)S(1)}, u32[]{:S(2)}, u32[]{:S(2)}) collective-permute-start(bf16[1,4,1,80,512]{4,3,2,1,0:T(8,128)(2,1)S(1)} %get-tuple-element.14), channel_id=1, source_target_pairs={{1,0},{2,1},{3,2},{5,4},{6,5},{7,6},{9,8},{10,9},{11,10},{13,12},{... | collective-permute-start | bytes 983048 | tf_op jit(solution)/shard_map/ppermute | solution.py:29
  100.9 283.5 %reduce-scatter.5.cloned.1.call-start = ((), (), s32[]{:S(2)}) async-start(), calls=%async_computation.6 | async-start | bytes 14598144 | tf_op jit(solution)/shard_map/reduce_scatter | solution.py:124
  119.6 3.8 copy-start
  126.4 6.1 %copy-start.3 = (bf16[2,2,2,80,13824]{4,3,2,1,0:T(8,128)(2,1)}, bf16[2,2,2,80,13824]{4,3,2,1,0:T(8,128)(2,1)S(1)}, u32[]{:S(2)}) copy-start(bf16[2,2,2,80,13824]{4,3,2,1,0:T(8,128)(2,1)S(1)} %slice_dynamic-update-slice_fusion.9) | copy-start | bytes 53084164
  384.4 75.5 %collective-permute-start.6 = (f32[432,256]{1,0:T(8,128)}, f32[432,256]{1,0:T(8,128)S(1)}, u32[]{:S(2)}, u32[]{:S(2)}) collective-permute-start(f32[432,256]{1,0:T(8,128)} %reduce-scatter.5.cloned.1.call-done), channel_id=1, source_target_pairs={{0,1},{1,0},{2,3},{3,2},{4,5},{5,4},{6,7},{7,6},{8,9},{9,8},{10,11... | collective-permute-start | bytes 1327112 | tf_op jit(solution)/shard_map/ppermute | solution.py:11
  461.0 16.7 %copy-start.5 = (f32[512]{0:T(512)S(1)}, f32[512]{0:T(512)}, u32[]{:S(2)}) copy-start(f32[512]{0:T(512)} %param.8) | copy-start | bytes 6148
  461.0 17.6 %collective-permute-start.7 = (f32[432,256]{1,0:T(8,128)S(1)}, f32[432,256]{1,0:T(8,128)S(1)}, u32[]{:S(2)}, u32[]{:S(2)}) collective-permute-start(f32[432,256]{1,0:T(8,128)S(1)} %add.59), channel_id=1, source_target_pairs={{0,2},{1,3},{2,0},{3,1},{4,6},{5,7},{6,4},{7,5},{8,10},{9,11},{10,... | collective-permute-start | bytes 1327112 | tf_op jit(solution)/shard_map/ppermute | solution.py:11
Sparse Core Ops, SparseCore 0:
  49.9 20.0 reduce-scatter.2
  101.1 18.5 all-gather.1
  141.6 242.8 reduce-scatter.4
